TPU v7x, 32 devices: a whole 2x2x4 slice. The times are simulated.
32 devices in a mesh: slab: 8 (over y, x, core), col: 4 (over z).
Axes of the slice: x: 2, y: 2, z: 4, core: 2. Of those that a mesh axis runs over, the one named last changes fastest.
Arguments:
- volume: bfloat16 [8, 512, 6144], P('slab', 'col'), may hold values from -6 to 6
- detector_row_weight: bfloat16 [8, 512], P(None, 'col'), may hold values from -0.25 to 0.25
- tile_bank: bfloat16 [4, 128, 128], replicated, may hold values from -0.5 to 0.5
- tile_class: int32 [8], replicated, may hold values from 0 to 3
- tile_shift: int32 [8], replicated, may hold values from 0 to 47
- owner_angle: int32 [8], replicated, may hold values from 0 to 7, each once
- measured: bfloat16 [8, 8, 6144], P('slab', None, 'col'), may hold values from -6 to 6
- window_slice: int32 [8], P('slab'), may hold values from -4 to 0
- window_col: int32 [8], P('slab'), may hold values from -32 to 16
Outputs:
- projection: bfloat16 [8, 8, 6144], P('slab', None, 'col')
- correlation: float32 [8, 4, 16], P('slab')
- shifts: float32 [2, 8], P(None, 'slab')
Inputs may be any that keep to these rules, and one draw needn't show every extreme that they name: `owner_angle`: every angle stands in exactly one slot.
All inputs are finite; a program needn't handle non-finite values.
Results may differ from a plain program's by a relative error of at most 0.0095.
Values may be sent and summed in bfloat16 or wider, within the bound.
A program may use at most 64 MiB of HBM per device.

v0:
```python
import math

import jax
import jax.numpy as jnp
from jax import lax
from jax.sharding import PartitionSpec as P

LAG = 32
WU = 16
LAGZ = 4
WZ = 4


def padded_2(block, sides, width):
    for axis, dim in sides:
        count = lax.axis_size(axis)
        forward = [(i, i + 1) for i in range(count - 1)]
        forward.append((count - 1, 0))
        backward = [(target, source) for source, target in forward]
        low = lax.ppermute(
            lax.slice_in_dim(block, block.shape[dim] - width, None, axis=dim), axis, forward
        )
        high = lax.ppermute(lax.slice_in_dim(block, 0, width, axis=dim), axis, backward)
        block = jnp.concatenate([low, block, high], axis=dim)
    return block


def correlate_one(owned_slot, padded_slot, start_slice, start_col, diagonal_mask, norm_factor):
    slice_count = owned_slot.shape[0]
    columns = owned_slot.shape[1]
    doubled = jnp.concatenate([padded_slot, padded_slot], axis=0)
    aligned = lax.dynamic_slice_in_dim(doubled, start_slice % slice_count, slice_count, 0)
    offsets = LAG + start_col + jnp.arange(WU, dtype=jnp.int32)

    def one_lag(position):
        piece = lax.dynamic_slice_in_dim(aligned, position, columns, 1)
        return lax.dot_general(
            owned_slot, piece, (((1,), (1,)), ((), ())), preferred_element_type=jnp.float32
        )

    gramians = lax.map(one_lag, offsets)
    return (
        jnp.einsum("bzy,azy->ab", gramians, diagonal_mask, precision=lax.Precision.HIGHEST)
        * norm_factor
    )


def local(
    volume,
    detector_row_weight,
    tile_bank,
    tile_class,
    tile_shift,
    owner_angle,
    measured,
    window_slice,
    window_col,
):
    slices, beam_rows, columns = volume.shape
    angles = detector_row_weight.shape[0]
    tile_size = tile_bank.shape[1]
    tile_count = columns // tile_size
    block_size = math.gcd(angles, 32)
    block_count = angles // block_size
    chosen = jnp.take(detector_row_weight, owner_angle, axis=0).reshape(
        block_count, block_size, beam_rows
    )
    openings = (tile_count - jnp.take(tile_shift, owner_angle)).reshape(block_count, block_size)
    classes = jnp.take(tile_class, owner_angle).reshape(block_count, block_size)

    def project_block(item):
        weights_block, openings_block, classes_block = item
        ray_sums = jnp.einsum(
            "ky,syx->ksx", weights_block, volume, preferred_element_type=jnp.float32
        ).astype(jnp.bfloat16)
        tiled = ray_sums.reshape(block_size, slices, tile_count, tile_size)
        doubled = jnp.concatenate([tiled, tiled], axis=2)
        rolled = jax.vmap(
            lambda planes, opening: lax.dynamic_slice_in_dim(planes, opening, tile_count, 1)
        )(doubled, openings_block)
        system_operators = jnp.take(tile_bank, classes_block, axis=0)
        return jnp.einsum(
            "kstc,kcd->kstd", rolled, system_operators, preferred_element_type=jnp.float32
        ).reshape(block_size, slices, columns)

    spread = lax.map(project_block, (chosen, openings, classes)).reshape(angles, slices, columns)
    moved = lax.all_to_all(
        spread.astype(jnp.bfloat16), "slab", split_axis=0, concat_axis=1, tiled=True
    )
    owned = (
        lax.psum_scatter(moved, "col", scatter_dimension=2, tiled=True)
        .astype(jnp.float32)
        .astype(jnp.bfloat16)
    )
    padded = padded_2(measured, (("col", 2),), LAG)
    slot_count, slice_grand_sum, quarter = owned.shape
    norm_factor = 1.0 / math.sqrt(slice_grand_sum * quarter * lax.axis_size("col"))
    slice_range = jnp.arange(slice_grand_sum, dtype=jnp.int32)
    lag_slices = jnp.arange(WZ, dtype=jnp.int32)
    lag_columns = jnp.arange(WU, dtype=jnp.int32)
    diagonal_mask = (
        slice_range[None, None, :]
        == (slice_range[None, :, None] + lag_slices[:, None, None]) % slice_grand_sum
    ).astype(jnp.float32)
    search_regions = jnp.stack(
        [
            correlate_one(
                owned[0], padded[0], window_slice[0], window_col[0], diagonal_mask, norm_factor
            )
        ]
    )
    totals = lax.psum(search_regions, "col")
    weight_grid = totals * totals
    along_slices = (window_slice[:, None] + lag_slices[None, :]).astype(jnp.float32) / LAGZ
    along_columns = (window_col[:, None] + lag_columns[None, :]).astype(jnp.float32) / LAG
    denominator = jnp.mean(weight_grid, axis=(1, 2)) + 1e-06
    shift_slices = jnp.mean(weight_grid * along_slices[:, :, None], axis=(1, 2)) / denominator
    shift_columns = jnp.mean(weight_grid * along_columns[:, None, :], axis=(1, 2)) / denominator
    return (owned, totals, jnp.stack([shift_slices, shift_columns]))


def solution(mesh):
    return jax.shard_map(
        local,
        mesh=mesh,
        in_specs=(
            P("slab", "col", None),
            P(None, "col"),
            P(),
            P(),
            P(),
            P(),
            P("slab", None, "col"),
            P("slab"),
            P("slab"),
        ),
        out_specs=(P("slab", None, "col"), P("slab", None, None), P(None, "slab")),
        check_vma=False,
    )
```

profile of v0, /device:TPU:0, one launch (start us, length us, event | category | flops | bytes accessed | tf_op | source)
XLA Modules:
  0.0 126.1 jit_solution(17264596399762606542)
XLA Ops:
  8.1 3.1 %collective-permute-start = (bf16[1,8,32]{2,1,0:T(8,128)(2,1)S(1)}, bf16[1,8,32]{2,1,0:T(8,128)(2,1)S(1)}, u32[]{:S(2)}, u32[]{:S(2)}) collective-permute-start(bf16[1,8,32]{2,1,0:T(8,128)(2,1)S(1)} %get-tuple-element.71), channel_id=1, source_target_pairs={{0,1},{1,2},{2,3},{3,0},{4,5},{5,6},{6,7},{7,4},{8,9},{9,10},{10,1... | collective-permute-start | bytes 1544 | tf_op jit(solution)/shard_map/ppermute | solution.py:20
  11.1 2.0 %collective-permute-start.1 = (bf16[1,8,32]{2,1,0:T(8,128)(2,1)S(1)}, bf16[1,8,32]{2,1,0:T(8,128)(2,1)S(1)}, u32[]{:S(2)}, u32[]{:S(2)}) collective-permute-start(bf16[1,8,32]{2,1,0:T(8,128)(2,1)S(1)} %get-tuple-element.70), channel_id=1, source_target_pairs={{1,0},{2,1},{3,2},{0,3},{5,4},{6,5},{7,6},{4,7},{9,8},{10,9},{11,1... | collective-permute-start | bytes 1544 | tf_op jit(solution)/shard_map/ppermute | solution.py:23
  13.8 1.3 %gather_fusion.3 = s32[8]{0:T(128)S(1)} fusion(s32[8]{0:T(128)} %param.17, s32[1024]{0:T(1024)S(1)} %pad_clamp_fusion.1), kind=kCustom, calls=%fused_computation.clone | custom fusion | bytes 96 | tf_op jit(solution)/shard_map/jit(_take)/gather | solution.py:68
  15.8 1.2 gather_fusion
  21.1 1.2 reduce.3
  23.0 3.9 %all-to-all-start = ((bf16[8,2,3072]{2,1,0:T(2,128)(2,1)}), bf16[8,2,3072]{2,1,0:T(2,128)(2,1)S(1)}, u32[]{:S(2)}, u32[]{:S(2)}) async-start(bf16[8,2,3072]{2,1,0:T(2,128)(2,1)} %reshape.200), calls=%async_computation | async-start | bytes 196608 | tf_op jit(solution)/shard_map/all_to_all | solution.py:87
  28.5 3.6 %all-to-all-done = bf16[8,2,3072]{2,1,0:T(2,128)(2,1)S(1)} async-done(((bf16[8,2,3072]{2,1,0:T(2,128)(2,1)}), bf16[8,2,3072]{2,1,0:T(2,128)(2,1)S(1)}, u32[]{:S(2)}, u32[]{:S(2)}) %all-to-all-start) | async-done | bytes 98336 | tf_op jit(solution)/shard_map/all_to_all | solution.py:87
  32.9 17.1 %reduce-scatter.2.cloned.1.call-done = bf16[1,8,1536]{2,1,0:T(8,128)(2,1)} async-done(((bf16[1,8,6144]{2,1,0:T(8,128)(2,1)}), bf16[1,8,1536]{2,1,0:T(8,128)(2,1)}) %reduce-scatter.2.cloned.1.call-update) | async-done | bytes 24592 | tf_op jit(solution)/shard_map/reduce_scatter | solution.py:91
  50.0 56.8 %while.2 = (s32[]{:T(128)}, f32[16,8,8]{2,1,0:T(8,128)S(1)}, s32[16]{0:T(128)S(1)}, bf16[8,1600]{1,0:T(8,128)(2,1)S(1)}, bf16[8,1536]{1,0:T(8,128)(2,1)}, /*index=5*/s32[]{:T(128)}, s32[]{:T(128)}, s32[]{:T(128)}) while((s32[]{:T(128)}, f32[16,8,8]{2,1,0:T(8,128)S(1)}, s32[16]{0:T(128)S(1)}, bf16[8,1600]{1,0:T(8,128)(2,1)S(1)}, ...), condition=%wide.region_2.4_spmd, body=%wide.region_1.3_spmd.sunk | while | flops 196613 | bytes 58251 | solution.py:41
  52.5 0.9 convolution_bitcast_fusion.3
  56.1 0.9 convolution_bitcast_fusion.3
  59.6 0.9 convolution_bitcast_fusion.3
  63.2 0.9 convolution_bitcast_fusion.3
  66.7 0.9 convolution_bitcast_fusion.3
  70.3 0.9 convolution_bitcast_fusion.3
  73.8 0.9 convolution_bitcast_fusion.3
  77.4 0.9 convolution_bitcast_fusion.3
  80.9 0.9 convolution_bitcast_fusion.3
  88.0 0.9 convolution_bitcast_fusion.3
  95.1 0.9 convolution_bitcast_fusion.3
  98.6 0.9 convolution_bitcast_fusion.3
  102.2 0.9 convolution_bitcast_fusion.3
  105.7 0.9 convolution_bitcast_fusion.3
  107.1 8.8 %psum.7 = f32[1,4,16]{2,1,0:T(4,128)S(1)} all-reduce(f32[1,4,16]{2,1,0:T(4,128)S(1)} %fusion.7), channel_id=1, replica_groups=mesh['slab'=8,'col'=4] {'col'}, use_global_device_ids=true, to_apply=%region_3.5 | all-reduce | flops 64 | bytes 512 | tf_op jit(solution)/shard_map/psum | solution.py:112
  (93 shorter events, 22.0 us)
Async XLA Ops:
  7.2 9.9 %copy-start = (bf16[1,128,6144]{2,1,0:T(8,128)(2,1)S(1)}, bf16[1,128,6144]{2,1,0:T(8,128)(2,1)}, u32[]{:S(2)}) copy-start(bf16[1,128,6144]{2,1,0:T(8,128)(2,1)} %param.13) | copy-start | bytes 4718596
  7.2 10.9 %copy-start.1 = (s32[8]{0:T(128)S(1)}, s32[8]{0:T(128)}, u32[]{:S(2)}) copy-start(s32[8]{0:T(128)} %param.16) | copy-start | bytes 100
  8.1 20.3 %collective-permute-start = (bf16[1,8,32]{2,1,0:T(8,128)(2,1)S(1)}, bf16[1,8,32]{2,1,0:T(8,128)(2,1)S(1)}, u32[]{:S(2)}, u32[]{:S(2)}) collective-permute-start(bf16[1,8,32]{2,1,0:T(8,128)(2,1)S(1)} %get-tuple-element.71), channel_id=1, source_target_pairs={{0,1},{1,2},{2,3},{3,0},{4,5},{5,6},{6,7},{7,4},{8,9},{9,10},{10,1... | collective-permute-start | bytes 1544 | tf_op jit(solution)/shard_map/ppermute | solution.py:20
  11.1 17.2 %collective-permute-start.1 = (bf16[1,8,32]{2,1,0:T(8,128)(2,1)S(1)}, bf16[1,8,32]{2,1,0:T(8,128)(2,1)S(1)}, u32[]{:S(2)}, u32[]{:S(2)}) collective-permute-start(bf16[1,8,32]{2,1,0:T(8,128)(2,1)S(1)} %get-tuple-element.70), channel_id=1, source_target_pairs={{1,0},{2,1},{3,2},{0,3},{5,4},{6,5},{7,6},{4,7},{9,8},{10,9},{11,1... | collective-permute-start | bytes 1544 | tf_op jit(solution)/shard_map/ppermute | solution.py:23
  17.4 2.2 %copy-start.2 = (bf16[4,128,128]{2,1,0:T(8,128)(2,1)S(1)}, bf16[4,128,128]{2,1,0:T(8,128)(2,1)}, u32[]{:S(2)}) copy-start(bf16[4,128,128]{2,1,0:T(8,128)(2,1)} %param.15) | copy-start | bytes 393220
  18.8 9.6 %copy-start.3 = (bf16[1,8,1536]{2,1,0:T(8,128)(2,1)S(1)}, bf16[1,8,1536]{2,1,0:T(8,128)(2,1)}, u32[]{:S(2)}) copy-start(bf16[1,8,1536]{2,1,0:T(8,128)(2,1)} %param.19) | copy-start | bytes 73732
  23.0 9.1 %all-to-all-start = ((bf16[8,2,3072]{2,1,0:T(2,128)(2,1)}), bf16[8,2,3072]{2,1,0:T(2,128)(2,1)S(1)}, u32[]{:S(2)}, u32[]{:S(2)}) async-start(bf16[8,2,3072]{2,1,0:T(2,128)(2,1)} %reshape.200), calls=%async_computation | async-start | bytes 196608 | tf_op jit(solution)/shard_map/all_to_all | solution.py:87
  26.9 23.1 %reduce-scatter.2.cloned.1.call-start = ((), (), s32[]{:S(2)}) async-start(), calls=%async_computation.2 | async-start | bytes 122880 | tf_op jit(solution)/shard_map/reduce_scatter | solution.py:91
  115.9 3.3 %copy-start.4 = (f32[1,4,16]{2,1,0:T(4,128)}, f32[1,4,16]{2,1,0:T(4,128)S(1)}, u32[]{:S(2)}) copy-start(f32[1,4,16]{2,1,0:T(4,128)S(1)} %psum.7) | copy-start | bytes 772
Sparse Core Ops, SparseCore 0:
  33.0 16.9 reduce-scatter.1
where the time goes:
time: 128 us; the launch traced here: 126 us
  loops' own time  31.1 us (24%)
  waiting for transfers between devices  20.7 us (16%)
  local copies, waits for them, and re-layouts  18.5 us (14%)
  between operations  17.5 us (14%)
  matrix products  15.8 us (12%)
  starting transfers between devices  9.06 us (7%)
  blocking collectives  8.82 us (7%)
  other arithmetic  4.45 us (3%)
    another operation x1, loops' own time, correlate_one(): gramians = lax.map(one_lag, offsets)  31.1 us
    reduce_scatter x1, waiting for transfers between devices, local(): lax.psum_scatter(moved, 'col', scatter_dimension=2, tiled=True)  17.1 us
    dot_general x16, matrix products, one_lag(): lax.dot_general(owned_slot, piece, (((1,), (1,)), ((), ())), preferred_el...  15 us
    dynamic_slice x16, local copies, waits for them, and re-layouts, correlate_one(): gramians = lax.map(one_lag, offsets)  9.41 us
    psum x1, blocking collectives, local(): totals = lax.psum(search_regions, 'col')  8.82 us
    all_to_all x1, starting transfers between devices, local(): lax.all_to_all(spread.astype(jnp.bfloat16), 'slab', split_axis=0, concat_...  3.94 us
    all_to_all x1, waiting for transfers between devices, local(): lax.all_to_all(spread.astype(jnp.bfloat16), 'slab', split_axis=0, concat_...  3.64 us
    ppermute x1, starting transfers between devices, padded_2(): lax.ppermute(lax.slice_in_dim(block, block.shape[dim] - width, None, axis...  3.05 us
  transfers between devices with their start and end apart: 4, of which 2 were waited for; matrix products, arithmetic and copies ran while one was open for 8% of the time, Pallas kernels for 0%

commit v1 on v0

v1 whole, which is shorter than its diff:
```python
import functools
import math

import jax
import jax.numpy as jnp
from jax import lax
from jax.experimental import pallas as pl
from jax.experimental.pallas import tpu as pltpu
from jax.sharding import PartitionSpec as P

LAG = 32
WU = 16
LAGZ = 4
WZ = 4
GROUP = 16
CHUNKS = 4
MESH = pl.DeviceIdType.MESH


def loop(count, body):
    if count <= 32:
        for i in range(count):
            body(i)
    else:
        lax.fori_loop(0, count, lambda i, c: (body(i), c)[1], 0)


def kernel(
    slabs,
    cols,
    volume,
    weight,
    bank,
    tile_class,
    tile_shift,
    owner,
    measured,
    window_slice,
    window_col,
    projection,
    correlation,
    shifts,
    vol,
    meas,
    ray,
    send,
    recv,
    halo,
    mrows,
    mturn,
    plane,
    stage,
    parts,
    load_sem,
    meas_sem,
    send_sem,
    recv_sem,
    halo_send,
    halo_recv,
    part_send,
    part_recv,
    out_sem,
):
    slab, col = lax.axis_index("slab"), lax.axis_index("col")
    devices = slabs * cols
    me = slab * cols + col
    angles = weight.shape[0]
    size = bank.shape[1]
    columns = volume.shape[2]
    tiles = columns // size
    quarter = tiles // cols
    span = ray.shape[0] // angles
    right, left = lax.rem(col + 1, cols), lax.rem(col + cols - 1, cols)

    width = columns // CHUNKS
    loads = [
        pltpu.make_async_copy(
            volume.at[0, :, pl.ds(i * width, width)],
            vol.at[:, pl.ds(i * width, width)],
            load_sem.at[i],
        )
        for i in range(CHUNKS)
    ]
    for load in loads:
        load.start()
    meas_copy = pltpu.make_async_copy(measured.at[0], meas, meas_sem)
    meas_copy.start()

    barrier = pltpu.get_barrier_semaphore()

    def greet(i):
        peer = lax.rem(me + 1 + i, devices)
        pl.semaphore_signal(
            barrier, inc=1, device_id=(peer // cols, lax.rem(peer, cols)), device_id_type=MESH
        )

    loop(devices - 1, greet)

    for i in range(CHUNKS):
        loads[i].wait()
        sums = jnp.dot(
            weight[...], vol[:, i * width : (i + 1) * width], preferred_element_type=jnp.float32
        )
        for t in range(width // size):
            piece = sums[:, t * size : (t + 1) * size]
            tile = i * (width // size) + t
            for at in range(tile, span, tiles):
                ray[pl.ds(at, angles, stride=span), :] = piece

    def gather(k):
        angle = owner[k]
        opening = angle * span + tiles - tile_shift[angle]
        for c in range(cols):
            rows = ray[pl.ds(opening + c * quarter, GROUP), :]
            send[k * cols + c] = rows.astype(jnp.bfloat16)

    loop(angles, gather)

    pl.semaphore_wait(barrier, devices - 1)

    meas_copy.wait()
    halos = [
        pltpu.make_async_remote_copy(
            src_ref=meas.at[:, pl.ds((quarter - 1) * size, size)],
            dst_ref=halo.at[0],
            send_sem=halo_send.at[0],
            recv_sem=halo_recv.at[0],
            device_id=(slab, right),
            device_id_type=MESH,
        ),
        pltpu.make_async_remote_copy(
            src_ref=meas.at[:, pl.ds(0, size)],
            dst_ref=halo.at[1],
            send_sem=halo_send.at[1],
            recv_sem=halo_recv.at[1],
            device_id=(slab, left),
            device_id_type=MESH,
        ),
    ]

    def pass_on(i):
        peer = lax.rem(me + 1 + i, devices)
        pltpu.make_async_remote_copy(
            src_ref=send.at[peer],
            dst_ref=recv.at[col * slabs + slab],
            send_sem=send_sem,
            recv_sem=recv_sem,
            device_id=(peer // cols, lax.rem(peer, cols)),
            device_id_type=MESH,
        ).start()

    loop(devices - 1, pass_on)
    pltpu.make_async_copy(send.at[me], recv.at[col * slabs + slab], recv_sem).start()
    for copy in halos:
        copy.start()

    depth = slabs * GROUP
    mrows[...] = jnp.zeros_like(mrows)

    def put(which, row, tile):
        for copy in range(3):
            start = (which * 3 + copy) * depth + row
            mrows[pl.ds(start, slabs, stride=GROUP), :] = tile

    for t in range(quarter):
        tile = meas[:, t * size : (t + 1) * size].astype(jnp.float32)
        put(0, t, tile)
        if t > 0:
            put(1, t - 1, tile)
        if t < quarter - 1:
            put(2, t + 1, tile)
    for copy in halos:
        copy.wait()
    put(2, 0, halo[0].astype(jnp.float32))
    put(1, quarter - 1, halo[1].astype(jnp.float32))
    first_slice = window_slice[0]
    for a in range(WZ):
        opening = (first_slice + a + slabs) * GROUP
        for which in range(3):
            rows = mrows[pl.ds(which * 3 * depth + opening, depth), :]
            mturn[pl.ds((a * 3 + which) * size, size), :] = rows.T.astype(jnp.bfloat16)

    matrix = bank[tile_class[owner[slab]]]
    pltpu.make_async_copy(recv, recv, recv_sem).wait()

    pieces = recv[...].reshape(devices * GROUP, size)
    spread = jnp.dot(pieces, matrix, preferred_element_type=jnp.float32)
    spread = spread.astype(jnp.bfloat16).astype(jnp.float32)
    total = spread[:depth]
    for j in range(1, cols):
        total = total + spread[j * depth : (j + 1) * depth]
    rounded = total.astype(jnp.bfloat16)
    plane[...] = rounded.astype(jnp.float32)

    products = jnp.dot(mturn[...], rounded, preferred_element_type=jnp.float32)
    ahead = lax.broadcasted_iota(jnp.int32, (size, size), 0) - lax.broadcasted_iota(
        jnp.int32, (size, size), 1
    )
    sublane = lax.broadcasted_iota(jnp.int32, (8, size), 0)
    row = lax.broadcasted_iota(jnp.int32, (8, size), 0)
    lags = jnp.zeros((8, size), jnp.float32)
    for a in range(WZ):
        same, after, before = (
            products[(a * 3 + which) * size : (a * 3 + which + 1) * size] for which in range(3)
        )
        block = jnp.where(
            ahead >= size // 2, before, jnp.where(ahead < -(size // 2), after, same)
        )
        lanes = block[:8]
        for i in range(1, size // 8):
            lanes = lanes + pltpu.roll(block[8 * i : 8 * i + 8], size - 8 * i, 1)
        for bit in (1, 2, 4):
            lanes = jnp.where((sublane & bit) != 0, pltpu.roll(lanes, size - bit, 1), lanes)
        summed = jnp.sum(lanes, axis=0, keepdims=True)
        lags = jnp.where(row == a, summed, lags)
    parts[col] = lags

    others = []
    for i in range(1, cols):
        copy = pltpu.make_async_remote_copy(
            src_ref=parts.at[col],
            dst_ref=parts.at[col],
            send_sem=part_send.at[i - 1],
            recv_sem=part_recv.at[i - 1],
            device_id=(slab, lax.rem(col + i, cols)),
            device_id_type=MESH,
        )
        copy.start()
        others.append(copy)

    for t in range(quarter):
        stage[:, t * size : (t + 1) * size] = plane[pl.ds(t, slabs, stride=GROUP), :].astype(
            jnp.bfloat16
        )
    out_copy = pltpu.make_async_copy(stage, projection.at[0], out_sem)
    out_copy.start()

    first_col = window_col[0]
    place = lax.broadcasted_iota(jnp.int32, (size, size), 0)
    lane = lax.broadcasted_iota(jnp.int32, (size, size), 1)
    chosen = ((place + lane + first_col) & (size - 1)) == 0
    chosen = jnp.where(chosen, 1.0, 0.0)

    for copy in others:
        copy.wait()
    whole = parts[0]
    for j in range(1, cols):
        whole = whole + parts[j]
    norm = 1.0 / math.sqrt(slabs * columns)
    window = (
        jnp.dot(
            whole, chosen, precision=lax.Precision.HIGHEST, preferred_element_type=jnp.float32
        )
        * norm
    )
    correlation[0] = window[:WZ, :WU]
    column = lax.broadcasted_iota(jnp.int32, (8, size), 1)
    inside = (row < WZ) & (column < WU)
    grid = jnp.where(inside, window * window, 0.0)
    along_slices = (first_slice + row).astype(jnp.float32) / LAGZ
    along_columns = (first_col + column).astype(jnp.float32) / LAG
    count = WZ * WU

    def mean(value):
        return jnp.sum(jnp.sum(value, axis=1, keepdims=True), axis=0, keepdims=True) / count

    denominator = mean(grid) + 1e-06
    shifts[0:1, :] = mean(grid * along_slices) / denominator
    shifts[1:2, :] = mean(grid * along_columns) / denominator

    out_copy.wait()
    sent = send.at[pl.ds(0, devices - 1)]
    pltpu.make_async_copy(sent, sent, send_sem).wait()


def local(slabs, cols, *args):
    volume, weight, bank = args[:3]
    measured = args[6]
    _, beam_rows, columns = volume.shape
    angles = weight.shape[0]
    size = bank.shape[1]
    tiles = columns // size
    devices = slabs * cols
    depth = slabs * GROUP
    span = 2 * tiles + 8
    any_space = pl.BlockSpec(memory_space=pl.ANY)
    vmem = pl.BlockSpec(memory_space=pltpu.VMEM)
    smem = pl.BlockSpec(memory_space=pltpu.SMEM)
    dma = pltpu.SemaphoreType.DMA
    return pl.pallas_call(
        functools.partial(kernel, slabs, cols),
        out_shape=(
            jax.ShapeDtypeStruct(measured.shape, jnp.bfloat16),
            jax.ShapeDtypeStruct((1, WZ, WU), jnp.float32),
            jax.ShapeDtypeStruct((2, 1), jnp.float32),
        ),
        in_specs=[any_space, vmem, vmem, smem, smem, smem, any_space, smem, smem],
        out_specs=(any_space, vmem, vmem),
        scratch_shapes=[
            pltpu.VMEM((beam_rows, columns), jnp.bfloat16),
            pltpu.VMEM(measured.shape[1:], jnp.bfloat16),
            pltpu.VMEM((angles * span, size), jnp.float32),
            pltpu.VMEM((devices, GROUP, size), jnp.bfloat16),
            pltpu.VMEM((devices, GROUP, size), jnp.bfloat16),
            pltpu.VMEM((2, slabs, size), jnp.bfloat16),
            pltpu.VMEM((9 * depth, size), jnp.float32),
            pltpu.VMEM((3 * WZ * size, depth), jnp.bfloat16),
            pltpu.VMEM((depth, size), jnp.float32),
            pltpu.VMEM(measured.shape[1:], jnp.bfloat16),
            pltpu.VMEM((cols, 8, size), jnp.float32),
            dma((CHUNKS,)),
            dma,
            dma,
            dma,
            dma((2,)),
            dma((2,)),
            dma((cols - 1,)),
            dma((cols - 1,)),
            dma,
        ],
        compiler_params=pltpu.CompilerParams(
            collective_id=0, has_side_effects=True, vmem_limit_bytes=60 * 1024 * 1024
        ),
    )(*args)


def solution(mesh):
    slabs, cols = mesh.shape["slab"], mesh.shape["col"]
    return jax.shard_map(
        functools.partial(local, slabs, cols),
        mesh=mesh,
        in_specs=(
            P("slab", "col", None),
            P(None, "col"),
            P(),
            P(),
            P(),
            P(),
            P("slab", None, "col"),
            P("slab"),
            P("slab"),
        ),
        out_specs=(P("slab", None, "col"), P("slab", None, None), P(None, "slab")),
        check_vma=False,
    )
```

time: 128 us -> 24.7 us (0.19); the launches traced: 126 us -> 24.4 us
  loops' own time: 31.1 us -> 0 us
  waiting for transfers between devices: 20.7 us -> 0 us
  Pallas kernels: 0 us -> 18.7 us
  matrix products: 15.8 us -> 0 us
  between operations: 17.5 us -> 1.93 us
  local copies, waits for them, and re-layouts: 18.5 us -> 3.81 us
  starting transfers between devices: 9.06 us -> 0 us
  blocking collectives: 8.82 us -> 0 us
  other arithmetic: 4.45 us -> 0 us
    another operation x1 -> x0, loops' own time: 31.1 us -> none  [correlate_one(): gramians = lax.map(one_lag, offsets)]
    pallas_call x0 -> x1, Pallas kernels: none -> 18.7 us  [local(): pl.pallas_call(functools.partial(kernel, slabs, cols), out_shape=(jax.Sha...]
    reduce_scatter x1 -> x0, waiting for transfers between devices: 17.1 us -> none  [local(): lax.psum_scatter(moved, 'col', scatter_dimension=2, tiled=True)]
    dot_general x19 -> x0, matrix products: 15.8 us -> none  [the longest x16 15 us: one_lag(): lax.dot_general(owned_slot, piece, (((1,), (1,)), ((), ())), preferred_el...]
    dynamic_slice x16 -> x0, local copies, waits for them, and re-layouts: 9.41 us -> none  [correlate_one(): gramians = lax.map(one_lag, offsets)]
    psum x1 -> x0, blocking collectives: 8.82 us -> none  [local(): totals = lax.psum(search_regions, 'col')]
    ppermute x2 -> x0, starting transfers between devices: 5.08 us -> none  [the longest x1 3.05 us: padded_2(): lax.ppermute(lax.slice_in_dim(block, block.shape[dim] - width, None, axis...]
    gather x5 -> x0, local copies, waits for them, and re-layouts: 4.62 us -> none  [the longest x1 1.29 us: local(): jnp.take(tile_shift, owner_angle)]
  transfers between devices with their start and end apart: 4 -> 0, of which waited for: 2 -> 0; matrix products, arithmetic and copies ran while one was open for 8% -> 0% of each run, Pallas kernels for 0% -> 0%
where the time goes in v1:
time: 24.7 us; the launch traced here: 24.4 us
  Pallas kernels  18.7 us (76%)
  local copies, waits for them, and re-layouts  3.81 us (15%)
  between operations  1.93 us (8%)
    pallas_call x1, Pallas kernels, local(): pl.pallas_call(functools.partial(kernel, slabs, cols), out_shape=(jax.Sha...  18.7 us
    unnamed x2, local copies, waits for them, and re-layouts  2.59 us
    pallas_call x1, local copies, waits for them, and re-layouts, local(): pl.pallas_call(functools.partial(kernel, slabs, cols), out_shape=(jax.Sha...  1.22 us

profile of v1, /device:TPU:0, one launch (start us, length us, event | category | flops | bytes accessed | tf_op | source)
XLA Modules:
  0.0 24.4 jit_solution(1356381013515768209)
XLA Ops:
  1.9 18.7 %shard_map.112 = (bf16[1,8,1536]{2,1,0:T(8,128)(2,1)}, f32[1,4,16]{2,1,0:T(4,128)}, f32[2,1]{1,0:T(2,128)}) custom-call(bf16[1,128,6144]{2,1,0:T(8,128)(2,1)} %volume.1, bf16[8,128]{1,0:T(8,128)(2,1)} %weight.1, bf16[4,128,128]{2,1,0:T(8,128)(2,1)} %bank.1, s32[8]{0:T(128)} %tile_class.1, s32[8]{0:T(128)} %tile_shift.1, s32[8]{0:T(128)} %owner.1, ...), custom_call_target="tpu_custom_call" | custom-call | tf_op jit(solution)/shard_map/pallas_call | solution.py:290
  20.6 1.2 %copy.12 = f32[2,1]{0,1:T(1,128)} copy(f32[2,1]{1,0:T(2,128)} %get-tuple-element.5) | data formatting | bytes 16 | tf_op jit(solution)/shard_map/pallas_call | solution.py:290
  21.8 1.3 %copy.17 = bf16[1,8,1536]{2,1,0:T(8,128)(2,1)} copy(bf16[1,8,1536]{2,1,0:T(8,128)(2,1)} %get-tuple-element.9) | data formatting | bytes 49152
  23.2 1.2 %copy.18 = f32[1,4,16]{2,1,0:T(4,128)} copy(f32[1,4,16]{2,1,0:T(4,128)} %get-tuple-element.10) | data formatting | bytes 512

commit v2 on v1

--- a/solution.py
+++ b/solution.py
@@ -29,17 +29,23 @@
     slabs,
     cols,
     volume,
+    weight_in,
+    bank_in,
+    class_in,
+    shift_in,
+    owner_in,
+    measured,
+    window_slice,
+    window_col,
+    stage,
+    parts,
+    chosen,
+    along,
     weight,
     bank,
     tile_class,
     tile_shift,
     owner,
-    measured,
-    window_slice,
-    window_col,
-    projection,
-    correlation,
-    shifts,
     vol,
     meas,
     ray,
@@ -49,9 +55,8 @@
     mrows,
     mturn,
     plane,
-    stage,
-    parts,
     load_sem,
+    small_sem,
     meas_sem,
     send_sem,
     recv_sem,
@@ -59,7 +64,6 @@
     halo_recv,
     part_send,
     part_recv,
-    out_sem,
 ):
     slab, col = lax.axis_index("slab"), lax.axis_index("col")
     devices = slabs * cols
@@ -81,8 +85,22 @@
         )
         for i in range(CHUNKS)
     ]
+    pairs = (
+        (weight_in, weight),
+        (owner_in, owner),
+        (shift_in, tile_shift),
+        (class_in, tile_class),
+        (bank_in, bank),
+    )
+    smalls = [
+        pltpu.make_async_copy(source, target, small_sem.at[i])
+        for i, (source, target) in enumerate(pairs)
+    ]
+    smalls[0].start()
     for load in loads:
         load.start()
+    for small in smalls[1:]:
+        small.start()
     meas_copy = pltpu.make_async_copy(measured.at[0], meas, meas_sem)
     meas_copy.start()
 
@@ -96,6 +114,7 @@
 
     loop(devices - 1, greet)
 
+    smalls[0].wait()
     for i in range(CHUNKS):
         loads[i].wait()
         sums = jnp.dot(
@@ -107,6 +126,8 @@
             for at in range(tile, span, tiles):
                 ray[pl.ds(at, angles, stride=span), :] = piece
 
+    smalls[1].wait()
+    smalls[2].wait()
     def gather(k):
         angle = owner[k]
         opening = angle * span + tiles - tile_shift[angle]
@@ -141,8 +162,8 @@
     def pass_on(i):
         peer = lax.rem(me + 1 + i, devices)
         pltpu.make_async_remote_copy(
-            src_ref=send.at[peer],
-            dst_ref=recv.at[col * slabs + slab],
+            src_ref=send.at[peer, pl.ds(0, quarter), :],
+            dst_ref=recv.at[col * slabs + slab, pl.ds(0, quarter), :],
             send_sem=send_sem,
             recv_sem=recv_sem,
             device_id=(peer // cols, lax.rem(peer, cols)),
@@ -150,7 +171,11 @@
         ).start()
 
     loop(devices - 1, pass_on)
-    pltpu.make_async_copy(send.at[me], recv.at[col * slabs + slab], recv_sem).start()
+    pltpu.make_async_copy(
+        send.at[me, pl.ds(0, quarter), :],
+        recv.at[col * slabs + slab, pl.ds(0, quarter), :],
+        recv_sem,
+    ).start()
     for copy in halos:
         copy.start()
 
@@ -180,8 +205,22 @@
             rows = mrows[pl.ds(which * 3 * depth + opening, depth), :]
             mturn[pl.ds((a * 3 + which) * size, size), :] = rows.T.astype(jnp.bfloat16)
 
+    first_col = window_col[0]
+    place = lax.broadcasted_iota(jnp.int32, (size, size), 0)
+    lane = lax.broadcasted_iota(jnp.int32, (size, size), 1)
+    norm = 1.0 / math.sqrt(slabs * columns)
+    inside = (((place + lane + first_col) & (size - 1)) == 0) & (lane < WU)
+    chosen[...] = jnp.where(inside, norm, 0.0)
+    row = lax.broadcasted_iota(jnp.int32, (8, size), 0)
+    column = lax.broadcasted_iota(jnp.int32, (8, size), 1)
+    along[0] = (first_slice + row).astype(jnp.float32) / LAGZ
+    along[1] = (first_col + column).astype(jnp.float32) / LAG
+
+    smalls[3].wait()
+    smalls[4].wait()
     matrix = bank[tile_class[owner[slab]]]
-    pltpu.make_async_copy(recv, recv, recv_sem).wait()
+    arrived = recv.at[:, pl.ds(0, quarter), :]
+    pltpu.make_async_copy(arrived, arrived, recv_sem).wait()
 
     pieces = recv[...].reshape(devices * GROUP, size)
     spread = jnp.dot(pieces, matrix, preferred_element_type=jnp.float32)
@@ -189,7 +228,8 @@
     total = spread[:depth]
     for j in range(1, cols):
         total = total + spread[j * depth : (j + 1) * depth]
-    rounded = total.astype(jnp.bfloat16)
+    filled = lax.broadcasted_iota(jnp.int32, (depth, size), 0) & (GROUP - 1)
+    rounded = jnp.where(filled < quarter, total, 0.0).astype(jnp.bfloat16)
     plane[...] = rounded.astype(jnp.float32)
 
     products = jnp.dot(mturn[...], rounded, preferred_element_type=jnp.float32)
@@ -197,7 +237,6 @@
         jnp.int32, (size, size), 1
     )
     sublane = lax.broadcasted_iota(jnp.int32, (8, size), 0)
-    row = lax.broadcasted_iota(jnp.int32, (8, size), 0)
     lags = jnp.zeros((8, size), jnp.float32)
     for a in range(WZ):
         same, after, before = (
@@ -232,45 +271,41 @@
         stage[:, t * size : (t + 1) * size] = plane[pl.ds(t, slabs, stride=GROUP), :].astype(
             jnp.bfloat16
         )
-    out_copy = pltpu.make_async_copy(stage, projection.at[0], out_sem)
-    out_copy.start()
-
-    first_col = window_col[0]
-    place = lax.broadcasted_iota(jnp.int32, (size, size), 0)
-    lane = lax.broadcasted_iota(jnp.int32, (size, size), 1)
-    chosen = ((place + lane + first_col) & (size - 1)) == 0
-    chosen = jnp.where(chosen, 1.0, 0.0)
-
     for copy in others:
         copy.wait()
+    sent = send.at[pl.ds(0, devices - 1), pl.ds(0, quarter), :]
+    pltpu.make_async_copy(sent, sent, send_sem).wait()
+
+
+def finish(stage, parts, chosen, along, projection, correlation, shifts, window, centre, sem):
+    first = pltpu.make_async_copy(stage, projection.at[0], sem.at[0])
+    first.start()
     whole = parts[0]
-    for j in range(1, cols):
+    for j in range(1, parts.shape[0]):
         whole = whole + parts[j]
-    norm = 1.0 / math.sqrt(slabs * columns)
-    window = (
-        jnp.dot(
-            whole, chosen, precision=lax.Precision.HIGHEST, preferred_element_type=jnp.float32
-        )
-        * norm
+    peaks = jnp.dot(
+        whole,
+        chosen[...],
+        precision=lax.Precision.HIGHEST,
+        preferred_element_type=jnp.float32,
     )
-    correlation[0] = window[:WZ, :WU]
-    column = lax.broadcasted_iota(jnp.int32, (8, size), 1)
-    inside = (row < WZ) & (column < WU)
-    grid = jnp.where(inside, window * window, 0.0)
-    along_slices = (first_slice + row).astype(jnp.float32) / LAGZ
-    along_columns = (first_col + column).astype(jnp.float32) / LAG
-    count = WZ * WU
+    window[0] = peaks[:WZ, :WU]
+    second = pltpu.make_async_copy(window, correlation, sem.at[1])
+    second.start()
+    grid = peaks * peaks
 
     def mean(value):
-        return jnp.sum(jnp.sum(value, axis=1, keepdims=True), axis=0, keepdims=True) / count
+        summed = jnp.sum(jnp.sum(value, axis=1, keepdims=True), axis=0, keepdims=True)
+        return summed / (WZ * WU)
 
     denominator = mean(grid) + 1e-06
-    shifts[0:1, :] = mean(grid * along_slices) / denominator
-    shifts[1:2, :] = mean(grid * along_columns) / denominator
-
-    out_copy.wait()
-    sent = send.at[pl.ds(0, devices - 1)]
-    pltpu.make_async_copy(sent, sent, send_sem).wait()
+    centre[:, 0:1] = mean(grid * along[0]) / denominator
+    centre[:, 1:2] = mean(grid * along[1]) / denominator
+    third = pltpu.make_async_copy(centre, shifts, sem.at[2])
+    third.start()
+    first.wait()
+    second.wait()
+    third.wait()
 
 
 def local(slabs, cols, *args):
@@ -285,30 +320,38 @@
     span = 2 * tiles + 8
     any_space = pl.BlockSpec(memory_space=pl.ANY)
     vmem = pl.BlockSpec(memory_space=pltpu.VMEM)
-    smem = pl.BlockSpec(memory_space=pltpu.SMEM)
     dma = pltpu.SemaphoreType.DMA
-    return pl.pallas_call(
+    block = measured.shape[1:]
+    scratch = [
+        pltpu.VMEM(weight.shape, jnp.bfloat16),
+        pltpu.VMEM(bank.shape, jnp.bfloat16),
+        pltpu.SMEM(args[3].shape, jnp.int32),
+        pltpu.SMEM(args[4].shape, jnp.int32),
+        pltpu.SMEM(args[5].shape, jnp.int32),
+        pltpu.VMEM((beam_rows, columns), jnp.bfloat16),
+        pltpu.VMEM(block, jnp.bfloat16),
+        pltpu.VMEM((angles * span, size), jnp.float32),
+        pltpu.VMEM((devices, GROUP, size), jnp.bfloat16),
+        pltpu.VMEM((devices, GROUP, size), jnp.bfloat16),
+        pltpu.VMEM((2, slabs, size), jnp.bfloat16),
+        pltpu.VMEM((9 * depth, size), jnp.float32),
+        pltpu.VMEM((3 * WZ * size, depth), jnp.bfloat16),
+        pltpu.VMEM((depth, size), jnp.float32),
+    ]
+    sums = pl.pallas_call(
         functools.partial(kernel, slabs, cols),
         out_shape=(
-            jax.ShapeDtypeStruct(measured.shape, jnp.bfloat16),
-            jax.ShapeDtypeStruct((1, WZ, WU), jnp.float32),
-            jax.ShapeDtypeStruct((2, 1), jnp.float32),
-        ),
-        in_specs=[any_space, vmem, vmem, smem, smem, smem, any_space, smem, smem],
-        out_specs=(any_space, vmem, vmem),
-        scratch_shapes=[
-            pltpu.VMEM((beam_rows, columns), jnp.bfloat16),
-            pltpu.VMEM(measured.shape[1:], jnp.bfloat16),
-            pltpu.VMEM((angles * span, size), jnp.float32),
-            pltpu.VMEM((devices, GROUP, size), jnp.bfloat16),
-            pltpu.VMEM((devices, GROUP, size), jnp.bfloat16),
-            pltpu.VMEM((2, slabs, size), jnp.bfloat16),
-            pltpu.VMEM((9 * depth, size), jnp.float32),
-            pltpu.VMEM((3 * WZ * size, depth), jnp.bfloat16),
-            pltpu.VMEM((depth, size), jnp.float32),
-            pltpu.VMEM(measured.shape[1:], jnp.bfloat16),
+            pltpu.VMEM(block, jnp.bfloat16),
             pltpu.VMEM((cols, 8, size), jnp.float32),
+            pltpu.VMEM((size, size), jnp.float32),
+            pltpu.VMEM((2, 8, size), jnp.float32),
+        ),
+        in_specs=[any_space] * 7 + [pl.BlockSpec(memory_space=pltpu.SMEM)] * 2,
+        out_specs=(vmem, vmem, vmem, vmem),
+        scratch_shapes=scratch
+        + [
             dma((CHUNKS,)),
+            dma((5,)),
             dma,
             dma,
             dma,
@@ -316,12 +359,30 @@
             dma((2,)),
             dma((cols - 1,)),
             dma((cols - 1,)),
-            dma,
         ],
         compiler_params=pltpu.CompilerParams(
-            collective_id=0, has_side_effects=True, vmem_limit_bytes=60 * 1024 * 1024
+            collective_id=0,
+            has_side_effects=True,
+            vmem_limit_bytes=60 * 2**20,
         ),
     )(*args)
+    projection, correlation, centre = pl.pallas_call(
+        finish,
+        out_shape=(
+            jax.ShapeDtypeStruct(measured.shape, jnp.bfloat16),
+            jax.ShapeDtypeStruct((1, WZ, WU), jnp.float32),
+            jax.ShapeDtypeStruct((1, 2), jnp.float32),
+        ),
+        in_specs=[vmem] * 4,
+        out_specs=(any_space, any_space, any_space),
+        scratch_shapes=[
+            pltpu.VMEM((1, WZ, WU), jnp.float32),
+            pltpu.VMEM((1, 2), jnp.float32),
+            dma((3,)),
+        ],
+        compiler_params=pltpu.CompilerParams(vmem_limit_bytes=16 * 2**20),
+    )(*sums)
+    return projection, correlation, centre.T
 
 
 def solution(mesh):

time: 24.7 us -> 19.3 us (0.78)
  local copies, waits for them, and re-layouts: 3.81 us -> 0 us
  Pallas kernels: 18.7 us -> 17.2 us
    unnamed x2 -> x0, local copies, waits for them, and re-layouts: 2.59 us -> none
    pallas_call x1 -> x2, Pallas kernels: 18.7 us -> 17.2 us  [the longest x1 16.4 us: local(): pl.pallas_call(functools.partial(kernel, slabs, cols), out_shape=(pltpu.V...]
    pallas_call x1 -> x0, local copies, waits for them, and re-layouts: 1.22 us -> none  [local(): pl.pallas_call(functools.partial(kernel, slabs, cols), out_shape=(jax.Sha...]
where the time goes in v2:
time: 19.3 us; the launch traced here: 19.1 us
  Pallas kernels  17.2 us (89%)
  between operations  1.93 us (10%)
    pallas_call x1, Pallas kernels, local(): pl.pallas_call(functools.partial(kernel, slabs, cols), out_shape=(pltpu.V...  16.4 us
    pallas_call x1, Pallas kernels, local(): pl.pallas_call(finish, out_shape=(jax.ShapeDtypeStruct(measured.shape, jn...  0.8 us

profile of v2, /device:TPU:0, one launch (start us, length us, event | category | flops | bytes accessed | tf_op | source)
XLA Modules:
  0.0 19.1 jit_solution(9783035765890648516)
XLA Ops:
  1.9 16.4 %shard_map.112 = (bf16[8,1536]{1,0:T(8,128)(2,1)S(1)}, f32[4,8,128]{2,1,0:T(8,128)S(1)}, f32[128,128]{1,0:T(8,128)S(1)}, f32[2,8,128]{2,1,0:T(8,128)S(1)}) custom-call(bf16[1,128,6144]{2,1,0:T(8,128)(2,1)} %volume.1, bf16[8,128]{1,0:T(8,128)(2,1)} %weight_in.1, bf16[4,128,128]{2,1,0:T(8,128)(2,1)} %bank_in.1, s32[8]{0:T(128)} %class_in.1, s32[8]{0:T(128)} %shift_in.1, ...), custom_call_target="tpu_custom_call" | custom-call | tf_op jit(solution)/shard_map/pallas_call | solution.py:341
  18.3 0.8 %shard_map.113 = (bf16[1,8,1536]{2,1,0:T(8,128)(2,1)}, f32[1,4,16]{2,1,0:T(4,128)}, f32[1,2]{1,0:T(1,128)}) custom-call(bf16[8,1536]{1,0:T(8,128)(2,1)S(1)} %get-tuple-element.10.stage, f32[4,8,128]{2,1,0:T(8,128)S(1)} %get-tuple-element.11.parts, f32[128,128]{1,0:T(8,128)S(1)} %get-tuple-element.12.chosen, f32[2,8,128]{2,1,0:T(8,128)S(1)} %get-tuple-element.13.along), custom_call_target="tpu_custom_call" | custom-call | tf_op jit(solution)/shard_map/pallas_call | solution.py:369

commit v3 on v2

--- a/solution.py
+++ b/solution.py
@@ -13,7 +13,7 @@
 LAGZ = 4
 WZ = 4
 GROUP = 16
-CHUNKS = 4
+CHUNKS = 2
 MESH = pl.DeviceIdType.MESH
 
 
@@ -76,6 +76,16 @@
     span = ray.shape[0] // angles
     right, left = lax.rem(col + 1, cols), lax.rem(col + cols - 1, cols)
 
+    barrier = pltpu.get_barrier_semaphore()
+
+    def greet(i):
+        peer = lax.rem(me + 1 + i, devices)
+        pl.semaphore_signal(
+            barrier, inc=1, device_id=(peer // cols, lax.rem(peer, cols)), device_id_type=MESH
+        )
+
+    loop(devices - 1, greet)
+
     width = columns // CHUNKS
     loads = [
         pltpu.make_async_copy(
@@ -104,15 +114,6 @@
     meas_copy = pltpu.make_async_copy(measured.at[0], meas, meas_sem)
     meas_copy.start()
 
-    barrier = pltpu.get_barrier_semaphore()
-
-    def greet(i):
-        peer = lax.rem(me + 1 + i, devices)
-        pl.semaphore_signal(
-            barrier, inc=1, device_id=(peer // cols, lax.rem(peer, cols)), device_id_type=MESH
-        )
-
-    loop(devices - 1, greet)
 
     smalls[0].wait()
     for i in range(CHUNKS):

time: 19.3 us -> 19.3 us (level)
  no operation moved by 1% of the time
where the time goes in v3:
time: 19.3 us; the launch traced here: 19.1 us
  Pallas kernels  17.1 us (89%)
  between operations  1.93 us (10%)
    pallas_call x1, Pallas kernels, local(): pl.pallas_call(functools.partial(kernel, slabs, cols), out_shape=(pltpu.V...  16.3 us
    pallas_call x1, Pallas kernels, local(): pl.pallas_call(finish, out_shape=(jax.ShapeDtypeStruct(measured.shape, jn...  0.8 us

profile of v3, /device:TPU:0, one launch (start us, length us, event | category | flops | bytes accessed | tf_op | source)
XLA Modules:
  0.0 19.1 jit_solution(16794328024195492083)
XLA Ops:
  1.9 16.3 %shard_map.112 = (bf16[8,1536]{1,0:T(8,128)(2,1)S(1)}, f32[4,8,128]{2,1,0:T(8,128)S(1)}, f32[128,128]{1,0:T(8,128)S(1)}, f32[2,8,128]{2,1,0:T(8,128)S(1)}) custom-call(bf16[1,128,6144]{2,1,0:T(8,128)(2,1)} %volume.1, bf16[8,128]{1,0:T(8,128)(2,1)} %weight_in.1, bf16[4,128,128]{2,1,0:T(8,128)(2,1)} %bank_in.1, s32[8]{0:T(128)} %class_in.1, s32[8]{0:T(128)} %shift_in.1, ...), custom_call_target="tpu_custom_call" | custom-call | tf_op jit(solution)/shard_map/pallas_call | solution.py:342
  18.3 0.8 %shard_map.113 = (bf16[1,8,1536]{2,1,0:T(8,128)(2,1)}, f32[1,4,16]{2,1,0:T(4,128)}, f32[1,2]{1,0:T(1,128)}) custom-call(bf16[8,1536]{1,0:T(8,128)(2,1)S(1)} %get-tuple-element.10.stage, f32[4,8,128]{2,1,0:T(8,128)S(1)} %get-tuple-element.11.parts, f32[128,128]{1,0:T(8,128)S(1)} %get-tuple-element.12.chosen, f32[2,8,128]{2,1,0:T(8,128)S(1)} %get-tuple-element.13.along), custom_call_target="tpu_custom_call" | custom-call | tf_op jit(solution)/shard_map/pallas_call | solution.py:370
